TPU v7x, 256 devices: a whole 4x4x8 slice. The times are simulated.
256 devices in a mesh: narrow: 8 (over x, z_lo), wide: 32 (over y, z_hi, core).
Axes of the slice: x: 4, y: 4, z: 8 (z_hi: 4, z_lo: 2; z = z_hi * 2 + z_lo), core: 2. Of those that a mesh axis runs over, the one named last changes fastest.
Arguments:
- basis: bfloat16 [128, 32, 512, 128], P(None, 'narrow', 'wide'), may hold values from -6 to 6
- rhs: bfloat16 [32, 512, 128], P('narrow', 'wide'), may hold values from -48 to 48
- coeffs: float32 [4, 32, 512, 128], P(None, 'narrow', 'wide'), may hold values from 0.25 to 4
- rows: int32 [4, 32, 512, 128], P(None, 'narrow', 'wide'), may hold values from 0 to 255
- signs: int32 [4, 32, 512, 128], P(None, 'narrow', 'wide'), may hold values from 0 to 1
- params: float32 [256, 4], P(('narrow', 'wide')), may hold values from 0.25 to 4
- order: int32 [256], replicated, may hold values from 0 to 255, each once
Outputs:
- fields: bfloat16 [256, 32, 512, 128], P(None, 'narrow', 'wide')
Inputs may be any that keep to these rules, and one draw needn't show every extreme that they name: `order`: each point number appears exactly once.
All inputs are finite; a program needn't handle non-finite values.
Results may differ from a plain program's by a relative error of at most 0.0056.
Values may be sent and summed in bfloat16 or wider, within the bound.
No kernel may reach another device: no remote copies, remote signals or barrier semaphores. Data moves between devices by JAX's collectives and lax.ppermute only.
A program may use at most 64 MiB of HBM per device.

v0:
```python
import jax
import jax.numpy as jnp
from jax import lax
from jax.sharding import PartitionSpec as P

K = 128
M = 1024
TERMS = 4
NNZ = 4


def extended(cells, sides, width):
    for axis, dim in sides:
        count = lax.axis_size(axis)
        ends = count - 1
        head = lax.slice_in_dim(cells, 0, width, axis=dim)
        tail = lax.slice_in_dim(cells, cells.shape[dim] - width, cells.shape[dim], axis=dim)
        cells = jnp.concatenate(
            [
                lax.ppermute(tail, axis, [(i, (i + 1) % count) for i in range(ends)]),
                cells,
                lax.ppermute(head, axis, [((i + 1) % count, i) for i in range(ends)]),
            ],
            axis=dim,
        )
    return cells


def column_products(sketched, sketched_rhs):
    dims = (((0,), (0,)), ((), ()))
    gram_matrix = lax.dot_general(
        sketched,
        sketched,
        dims,
        precision=lax.Precision.HIGHEST,
        preferred_element_type=jnp.float32,
    )
    projected = lax.dot_general(
        sketched,
        sketched_rhs,
        dims,
        precision=lax.Precision.HIGHEST,
        preferred_element_type=jnp.float32,
    )
    return (gram_matrix, projected)


def solve_points(point_params, gram_matrix, projected):
    gram_blocks = gram_matrix.reshape(TERMS, K, TERMS, K)
    proj_blocks = projected.reshape(TERMS, K)
    pair_weight = point_params[:, :, None] * point_params[:, None, :]
    normal = jnp.einsum("pqr,qirj->pij", pair_weight, gram_blocks, precision=lax.Precision.HIGHEST)
    right_side = jnp.einsum("pq,qi->pi", point_params, proj_blocks, precision=lax.Precision.HIGHEST)
    lower_factor = jnp.linalg.cholesky(normal)
    forward = lax.linalg.triangular_solve(
        lower_factor, right_side[:, :, None], left_side=True, lower=True
    )
    solved = lax.linalg.triangular_solve(
        lower_factor, forward, left_side=True, lower=True, transpose_a=True
    )
    return solved[:, :, 0]


def per_device(basis, rhs, coeffs, rows, signs, params, order):
    cell_count = basis.shape[1] * basis.shape[2] * basis.shape[3]
    padded = extended(basis, (("narrow", 1), ("wide", 2)), 1).astype(jnp.float32)
    centre = padded[:, 1:-1, 1:-1, :]
    along_x = 2.0 * centre - padded[:, :-2, 1:-1, :] - padded[:, 2:, 1:-1, :]
    along_y = 2.0 * centre - padded[:, 1:-1, :-2, :] - padded[:, 1:-1, 2:, :]
    z_padded = jnp.pad(centre, ((0, 0), (0, 0), (0, 0), (1, 1)))
    along_z = 2.0 * centre - z_padded[..., :-2] - z_padded[..., 2:]
    terms = jnp.stack(
        [coeffs[0] * centre, coeffs[1] * along_x, coeffs[2] * along_y, coeffs[3] * along_z]
    )
    terms = terms.astype(jnp.bfloat16).reshape(TERMS * K, cell_count)
    row_block = M // NNZ
    flat_rows = rows.reshape(NNZ, cell_count)
    sign_values = ((2 * signs - 1).astype(jnp.float32) * 0.5).reshape(NNZ, cell_count)
    flat_rhs = rhs.reshape(cell_count)
    block_cells = max(min(1024, cell_count), cell_count // 16)
    block_count = cell_count // block_cells
    row_slots = lax.broadcasted_iota(jnp.int32, (1, row_block, 1), 1)

    def accumulate(turn_index, carry):
        sketch_sum, rhs_sum = carry
        offset = turn_index * block_cells
        hashed_rows = lax.dynamic_slice_in_dim(flat_rows, offset, block_cells, 1)
        hashed_signs = lax.dynamic_slice_in_dim(sign_values, offset, block_cells, 1)
        hashed = jnp.where(row_slots == hashed_rows[:, None, :], hashed_signs[:, None, :], 0.0)
        hashed = hashed.astype(jnp.bfloat16).reshape(M, block_cells)
        columns = lax.dynamic_slice_in_dim(terms, offset, block_cells, 1)
        sketch_sum = sketch_sum + lax.dot_general(
            hashed, columns, (((1,), (1,)), ((), ())), preferred_element_type=jnp.float32
        )
        source = lax.dynamic_slice_in_dim(flat_rhs, offset, block_cells, 0)
        rhs_sum = rhs_sum + jnp.dot(hashed, source, preferred_element_type=jnp.float32)
        return (sketch_sum, rhs_sum)

    start = (jnp.zeros((M, TERMS * K), jnp.float32), jnp.zeros((M,), jnp.float32))
    sketched, sketched_rhs = lax.fori_loop(0, block_count, accumulate, start)
    sketched, sketched_rhs = lax.psum((sketched, sketched_rhs), ("narrow", "wide"))
    gram_matrix, projected = column_products(sketched, sketched_rhs)
    own_coef = solve_points(params, gram_matrix, projected).astype(jnp.bfloat16)
    all_coef = lax.all_gather(own_coef, ("narrow", "wide"), axis=0, tiled=True)
    point_total = all_coef.shape[0]
    picker = (order[:, None] == lax.broadcasted_iota(jnp.int32, (1, point_total), 1)).astype(
        jnp.bfloat16
    )
    picked = jnp.dot(picker, all_coef, preferred_element_type=jnp.float32).astype(jnp.bfloat16)
    fields = jnp.dot(picked, basis.reshape(K, cell_count), preferred_element_type=jnp.float32)
    return fields.astype(jnp.bfloat16).reshape(
        point_total, basis.shape[1], basis.shape[2], basis.shape[3]
    )


def solution(mesh):
    in_specs = (
        P(None, "narrow", "wide", None),
        P("narrow", "wide", None),
        P(None, "narrow", "wide", None),
        P(None, "narrow", "wide", None),
        P(None, "narrow", "wide", None),
        P(("narrow", "wide"), None),
        P(),
    )
    out_specs = P(None, "narrow", "wide", None)
    return jax.shard_map(
        per_device, mesh=mesh, in_specs=in_specs, out_specs=out_specs, check_vma=False
    )
```

profile of v0, /device:TPU:1, one launch (start us, length us, event | category | flops | bytes accessed | tf_op | source)
XLA Modules:
  0.0 799.9 jit_solution(9524437281529108941)
XLA Ops:
  9.0 5.1 collective-permute-start
  15.8 8.4 %collective-permute-done = bf16[128,1,16,128]{3,0,2,1:T(8,128)(2,1)} collective-permute-done((bf16[128,1,16,128]{3,0,2,1:T(8,128)(2,1)}, bf16[128,1,16,128]{3,0,2,1:T(8,128)(2,1)}, u32[]{:S(2)}, u32[]{:S(2)}) %collective-permute-start) | collective-permute-done | bytes 524320 | tf_op jit(solution)/shard_map/ppermute | solution.py:20
  26.9 10.0 %collective-permute-done.1 = bf16[128,1,16,128]{3,0,2,1:T(8,128)(2,1)S(1)} collective-permute-done((bf16[128,1,16,128]{3,0,2,1:T(8,128)(2,1)S(1)}, bf16[128,1,16,128]{3,0,2,1:T(8,128)(2,1)S(1)}, u32[]{:S(2)}, u32[]{:S(2)}) %collective-permute-start.1) | collective-permute-done | bytes 524320 | tf_op jit(solution)/shard_map/ppermute | solution.py:22
  37.0 6.3 collective-permute-start.2
  46.0 7.4 collective-permute-done.3
  63.0 12.0 %copy.17 = bf16[4,128,4,16,128]{4,3,2,1,0:T(8,128)(2,1)} copy(bf16[4,128,4,16,128]{4,1,3,2,0:T(8,128)(2,1)} %pad_maximum_fusion) | data formatting | bytes 16777216 | tf_op jit(solution)/shard_map/stack | solution.py:72
  75.1 13.3 %convert_element_type.36 = bf16[512,8192]{1,0:T(8,128)(2,1)} reshape(bf16[4,128,4,16,128]{4,3,2,1,0:T(8,128)(2,1)} %copy.17) | data formatting | bytes 16777216 | tf_op jit(solution)/shard_map/convert_element_type | solution.py:75
  88.4 50.1 %while.16 = (s32[]{:T(128)}, f32[1024,512]{1,0:T(8,128)}, f32[1024]{0:T(1024)S(1)}, s32[4,8192]{1,0:T(4,128)S(1)}, bf16[4,8192]{1,0:T(4,128)(2,1)S(1)}, /*index=...) while((s32[]{:T(128)}, f32[1024,512]{1,0:T(8,128)}, ...), condition=%wide.region_1.2_spmd.clone, body=%wide.region_0.1_spmd.clone.sunk | while | flops 1078986752 | bytes 11651254 | solution.py:100
  88.8 3.8 select_add_fusion.4
  94.5 4.5 select_add_fusion.4
  100.8 4.5 select_add_fusion.4
  107.2 4.5 select_add_fusion.4
  113.5 4.5 select_add_fusion.4
  119.9 4.5 select_add_fusion.4
  126.2 4.5 select_add_fusion.4
  132.6 4.5 select_add_fusion.4
  138.6 78.1 %psum.15 = f32[1024]{0:T(1024)S(1)} all-reduce(f32[1024]{0:T(1024)S(1)} %get-tuple-element.146), channel_id=1, replica_groups=mesh['narrow'=8,'wide'=32] {'narrow','wide'}, use_global_device_ids=true, to_apply=%region_5.6 | all-reduce | flops 1024 | bytes 8192 | tf_op jit(solution)/shard_map/psum | solution.py:101
  216.7 186.0 %all-reduce.3.cloned.1.call-done = f32[1024,512]{1,0:T(8,128)} async-done(((f32[1024,512]{1,0:T(8,128)}), f32[1024,512]{1,0:T(8,128)}) %all-reduce.3.cloned.1.call-update) | async-done | bytes 2097168 | tf_op jit(solution)/shard_map/psum | solution.py:101
  402.7 5.7 fusion.36
  412.7 11.7 %custom-call.9 = f32[1,128,128]{2,1,0:T(8,128)S(1)} custom-call(f32[1,128,128]{2,1,0:T(8,128)S(1)} %fusion.29), custom_call_target="Cholesky" | custom-call | tf_op jit(solution)/shard_map/jit(cholesky)/cholesky | solution.py:54
  425.7 9.8 %custom-call.10 = f32[1,1,128,128]{2,3,1,0:T(8,128)S(1)} custom-call(f32[1,1,128,128]{3,2,1,0:T(8,128)S(1)} %fusion.24), custom_call_target="InvertDiagBlocksLowerTriangular" | custom-call | tf_op jit(solution)/shard_map/triangular_solve | solution.py:58
  437.5 344.6 %all-gather.1 = bf16[256,1,128]{2,1,0:T(2,128)(2,1)S(1)} all-gather(bf16[1,1,128]{2,1,0:T(2,128)(2,1)S(1)} %fusion.21), channel_id=2, replica_groups=mesh['narrow'=8,'wide'=32] {'narrow','wide'}, dimensions={0}, use_global_device_ids=true | all-gather | bytes 65792 | tf_op jit(solution)/shard_map/all_gather | solution.py:104
  782.1 5.6 fusion.13
  787.7 5.4 copy.27
  (121 shorter events, 40.8 us)
Async XLA Ops:
  6.5 18.8 %copy-start.1 = (bf16[128,4,16,128]{3,2,1,0:T(8,128)(2,1)S(1)}, bf16[128,4,16,128]{3,2,1,0:T(8,128)(2,1)}, u32[]{:S(2)}) copy-start(bf16[128,4,16,128]{3,2,1,0:T(8,128)(2,1)} %param.9) | copy-start | bytes 6291460
  6.5 9.1 %copy-start.2 = (s32[4,4,16,128]{3,2,1,0:T(8,128)S(1)}, s32[4,4,16,128]{3,2,1,0:T(8,128)}, u32[]{:S(2)}) copy-start(s32[4,4,16,128]{3,2,1,0:T(8,128)} %param.13) | copy-start | bytes 393220
  6.5 9.2 %copy-start.3 = (s32[4,4,16,128]{3,2,1,0:T(8,128)S(1)}, s32[4,4,16,128]{3,2,1,0:T(8,128)}, u32[]{:S(2)}) copy-start(s32[4,4,16,128]{3,2,1,0:T(8,128)} %param.12) | copy-start | bytes 393220
  6.5 396.1 %all-reduce.3.cloned.1.call-start = ((), (), s32[]{:S(2)}) async-start(), calls=%async_computation | async-start | bytes 4194304 | tf_op jit(solution)/shard_map/psum | solution.py:101
  9.0 15.3 %collective-permute-start = (bf16[128,1,16,128]{3,0,2,1:T(8,128)(2,1)}, bf16[128,1,16,128]{3,0,2,1:T(8,128)(2,1)}, u32[]{:S(2)}, u32[]{:S(2)}) collective-permute-start(bf16[128,1,16,128]{3,0,2,1:T(8,128)(2,1)} %copy.40), channel_id=1, source_target_pairs={{0,32},{32,64},{64,96},{96,128},{128,160},{160,192},{192,224},{1,3... | collective-permute-start | bytes 1572872 | tf_op jit(solution)/shard_map/ppermute | solution.py:20
  14.3 22.6 %collective-permute-start.1 = (bf16[128,1,16,128]{3,0,2,1:T(8,128)(2,1)S(1)}, bf16[128,1,16,128]{3,0,2,1:T(8,128)(2,1)S(1)}, u32[]{:S(2)}, u32[]{:S(2)}) collective-permute-start(bf16[128,1,16,128]{3,0,2,1:T(8,128)(2,1)S(1)} %copy.41), channel_id=1, source_target_pairs={{32,0},{64,32},{96,64},{128,96},{160,128},{192,160},{224,192},{33,... | collective-permute-start | bytes 1572872 | tf_op jit(solution)/shard_map/ppermute | solution.py:22
  25.4 19.9 %copy-start.4 = (f32[4,4,16,128]{3,2,1,0:T(8,128)S(1)}, f32[4,4,16,128]{3,2,1,0:T(8,128)}, u32[]{:S(2)}) copy-start(f32[4,4,16,128]{3,2,1,0:T(8,128)} %param.11) | copy-start | bytes 393220
  37.0 8.9 %collective-permute-start.2 = (bf16[128,6,1,128]{3,0,2,1:T(8,128)(2,1)S(1)}, bf16[128,6,1,128]{3,0,2,1:T(8,128)(2,1)S(1)}, u32[]{:S(2)}, u32[]{:S(2)}) collective-permute-start(bf16[128,6,1,128]{3,0,2,1:T(8,128)(2,1)S(1)} %get-tuple-element.191), channel_id=1, source_target_pairs={{0,1},{1,2},{2,3},{3,4},{4,5},{5,6},{6,7},{7,8},{8,9},{9,10},{10,1... | collective-permute-start | bytes 589832 | tf_op jit(solution)/shard_map/ppermute | solution.py:20
  43.3 10.0 %collective-permute-start.3 = (bf16[128,6,1,128]{3,0,2,1:T(8,128)(2,1)S(1)}, bf16[128,6,1,128]{3,0,2,1:T(8,128)(2,1)S(1)}, u32[]{:S(2)}, u32[]{:S(2)}) collective-permute-start(bf16[128,6,1,128]{3,0,2,1:T(8,128)(2,1)S(1)} %get-tuple-element.192), channel_id=1, source_target_pairs={{1,0},{2,1},{3,2},{4,3},{5,4},{6,5},{7,6},{8,7},{9,8},{10,9},{11,1... | collective-permute-start | bytes 589832 | tf_op jit(solution)/shard_map/ppermute | solution.py:22
  88.4 50.1 %copy-start.5 = (f32[1,4]{1,0:T(1,128)S(1)}, f32[1,4]{1,0:T(1,128)}, u32[]{:S(2)}) copy-start(f32[1,4]{1,0:T(1,128)} %param.14) | copy-start | bytes 52
  408.4 27.2 %copy-start = (f32[1024,512]{1,0:T(8,128)S(1)}, f32[1024,512]{1,0:T(8,128)}, u32[]{:S(2)}) copy-start(f32[1024,512]{1,0:T(8,128)} %all-reduce.3.cloned.1.call-done) | copy-start | bytes 6291460
  408.4 373.7 %copy-start.6 = (s32[256]{0:T(256)S(1)}, s32[256]{0:T(256)}, u32[]{:S(2)}) copy-start(s32[256]{0:T(256)} %param.15) | copy-start | bytes 3076
Sparse Core Ops, SparseCore 0:
  138.6 263.9 all-reduce.2
where the time goes:
time: 801 us; the launch traced here: 800 us
  blocking collectives  423 us (53%)
  waiting for transfers between devices  213 us (27%)
  matrix products  56.7 us (7%)
  local copies, waits for them, and re-layouts  43.4 us (5%)
  other arithmetic  36 us (4%)
  starting transfers between devices  14.7 us (2%)
  between operations  13.6 us (2%)
    all_gather x1, blocking collectives, per_device(): all_coef = lax.all_gather(own_coef, ('narrow', 'wide'), axis=0, tiled=True)  345 us
    psum x1, waiting for transfers between devices, per_device(): lax.psum((sketched, sketched_rhs), ('narrow', 'wide'))  186 us
    psum x1, blocking collectives, per_device(): lax.psum((sketched, sketched_rhs), ('narrow', 'wide'))  78.1 us
    dot_general x8, matrix products, accumulate(): lax.dot_general(hashed, columns, (((1,), (1,)), ((), ())), preferred_elem...  35.6 us
    ppermute x2, waiting for transfers between devices, extended(): lax.ppermute(head, axis, [((i + 1) % count, i) for i in range(ends)])  17.4 us
  transfers between devices with their start and end apart: 5, of which 5 were waited for; matrix products, arithmetic and copies ran while one was open for 0% of the time, Pallas kernels for 0%

commit v1 on v0

--- a/solution.py
+++ b/solution.py
@@ -98,7 +98,7 @@
 
     start = (jnp.zeros((M, TERMS * K), jnp.float32), jnp.zeros((M,), jnp.float32))
     sketched, sketched_rhs = lax.fori_loop(0, block_count, accumulate, start)
-    sketched, sketched_rhs = lax.psum((sketched, sketched_rhs), ("narrow", "wide"))
+    sketched, sketched_rhs = lax.psum(lax.psum((sketched, sketched_rhs), "wide"), "narrow")
     gram_matrix, projected = column_products(sketched, sketched_rhs)
     own_coef = solve_points(params, gram_matrix, projected).astype(jnp.bfloat16)
     all_coef = lax.all_gather(own_coef, ("narrow", "wide"), axis=0, tiled=True)

time: 801 us -> 943 us (1.18)
  waiting for transfers between devices: 213 us -> 342 us
  blocking collectives: 423 us -> 435 us
    psum x1 -> x2, waiting for transfers between devices: 186 us -> 316 us  [the longest x1 292 us: per_device(): lax.psum((sketched, sketched_rhs), 'wide')]
    psum x1 -> x2, blocking collectives: 78.1 us -> 88.8 us  [the longest x1 71.2 us: per_device(): lax.psum((sketched, sketched_rhs), 'wide')]
  transfers between devices with their start and end apart: 5 -> 6, of which waited for: 5 -> 6; matrix products, arithmetic and copies ran while one was open for 0% -> 0% of each run, Pallas kernels for 0% -> 0%
where the time goes in v1:
time: 943 us; the launch traced here: 942 us
  blocking collectives  435 us (46%)
  waiting for transfers between devices  342 us (36%)
  matrix products  56.7 us (6%)
  local copies, waits for them, and re-layouts  43.4 us (5%)
  other arithmetic  36 us (4%)
  starting transfers between devices  14.7 us (2%)
  between operations  13.7 us (1%)
    all_gather x1, blocking collectives, per_device(): all_coef = lax.all_gather(own_coef, ('narrow', 'wide'), axis=0, tiled=True)  346 us
    psum x1, waiting for transfers between devices, per_device(): lax.psum((sketched, sketched_rhs), 'wide')  292 us
    psum x1, blocking collectives, per_device(): lax.psum((sketched, sketched_rhs), 'wide')  71.2 us
    dot_general x8, matrix products, accumulate(): lax.dot_general(hashed, columns, (((1,), (1,)), ((), ())), preferred_elem...  35.6 us
    psum x1, waiting for transfers between devices, per_device(): lax.psum(lax.psum((sketched, sketched_rhs), 'wide'), 'narrow')  23.6 us
  transfers between devices with their start and end apart: 6, of which 6 were waited for; matrix products, arithmetic and copies ran while one was open for 0% of the time, Pallas kernels for 0%

profile of v1, /device:TPU:1, one launch (start us, length us, event | category | flops | bytes accessed | tf_op | source)
XLA Modules:
  0.0 942.0 jit_solution(2425200954049439084)
XLA Ops:
  9.0 5.2 collective-permute-start
  15.9 8.4 collective-permute-done
  26.9 10.0 %collective-permute-done.1 = bf16[128,1,16,128]{3,0,2,1:T(8,128)(2,1)S(1)} collective-permute-done((bf16[128,1,16,128]{3,0,2,1:T(8,128)(2,1)S(1)}, bf16[128,1,16,128]{3,0,2,1:T(8,128)(2,1)S(1)}, u32[]{:S(2)}, u32[]{:S(2)}) %collective-permute-start.1) | collective-permute-done | bytes 524320 | tf_op jit(solution)/shard_map/ppermute | solution.py:22
  37.0 6.3 collective-permute-start.2
  46.0 7.4 collective-permute-done.3
  63.0 12.0 %copy.17 = bf16[4,128,4,16,128]{4,3,2,1,0:T(8,128)(2,1)} copy(bf16[4,128,4,16,128]{4,1,3,2,0:T(8,128)(2,1)} %pad_maximum_fusion) | data formatting | bytes 16777216 | tf_op jit(solution)/shard_map/stack | solution.py:72
  75.1 13.3 %convert_element_type.36 = bf16[512,8192]{1,0:T(8,128)(2,1)} reshape(bf16[4,128,4,16,128]{4,3,2,1,0:T(8,128)(2,1)} %copy.17) | data formatting | bytes 16777216 | tf_op jit(solution)/shard_map/convert_element_type | solution.py:75
  88.4 50.1 %while.16 = (s32[]{:T(128)}, f32[1024,512]{1,0:T(8,128)}, f32[1024]{0:T(1024)S(1)}, s32[4,8192]{1,0:T(4,128)S(1)}, bf16[4,8192]{1,0:T(4,128)(2,1)S(1)}, /*index=...) while((s32[]{:T(128)}, f32[1024,512]{1,0:T(8,128)}, ...), condition=%wide.region_1.2_spmd.clone, body=%wide.region_0.1_spmd.clone.sunk | while | flops 1078986752 | bytes 11651254 | solution.py:100
  94.5 4.5 select_add_fusion.4
  100.8 4.5 select_add_fusion.4
  113.5 4.5 select_add_fusion.4
  119.9 4.5 select_add_fusion.4
  126.2 4.5 select_add_fusion.4
  132.6 4.5 select_add_fusion.4
  138.5 292.2 %all-reduce.4.cloned.1.call-done = f32[1024,512]{1,0:T(8,128)} async-done(((f32[1024,512]{1,0:T(8,128)}), f32[1024,512]{1,0:T(8,128)}) %all-reduce.4.cloned.1.call-update) | async-done | bytes 2097168 | tf_op jit(solution)/shard_map/psum | solution.py:101
  430.9 71.2 %psum.30 = f32[1024]{0:T(1024)S(1)} all-reduce(f32[1024]{0:T(1024)S(1)} %get-tuple-element.146), channel_id=1, replica_groups=mesh['narrow'=8,'wide'=32] {'wide'}, use_global_device_ids=true, to_apply=%region_6.7 | all-reduce | flops 1024 | bytes 8192 | tf_op jit(solution)/shard_map/psum | solution.py:101
  502.1 17.6 %psum.31 = f32[1024]{0:T(1024)S(1)} all-reduce(f32[1024]{0:T(1024)S(1)} %psum.30), channel_id=1, replica_groups=mesh['narrow'=8,'wide'=32] {'narrow'}, use_global_device_ids=true, to_apply=%region_7.8 | all-reduce | flops 1024 | bytes 8192 | tf_op jit(solution)/shard_map/psum | solution.py:101
  519.7 23.6 %all-reduce.6.cloned.1.call-done = f32[1024,512]{1,0:T(8,128)} async-done(((f32[1024,512]{1,0:T(8,128)}), f32[1024,512]{1,0:T(8,128)}) %all-reduce.6.cloned.1.call-update) | async-done | bytes 2097168 | tf_op jit(solution)/shard_map/psum | solution.py:101
  543.3 5.7 fusion.36
  553.3 11.7 %custom-call.9 = f32[1,128,128]{2,1,0:T(8,128)S(1)} custom-call(f32[1,128,128]{2,1,0:T(8,128)S(1)} %fusion.29), custom_call_target="Cholesky" | custom-call | tf_op jit(solution)/shard_map/jit(cholesky)/cholesky | solution.py:54
  566.3 9.8 %custom-call.10 = f32[1,1,128,128]{2,3,1,0:T(8,128)S(1)} custom-call(f32[1,1,128,128]{3,2,1,0:T(8,128)S(1)} %fusion.24), custom_call_target="InvertDiagBlocksLowerTriangular" | custom-call | tf_op jit(solution)/shard_map/triangular_solve | solution.py:58
  578.1 346.1 %all-gather.1 = bf16[256,1,128]{2,1,0:T(2,128)(2,1)S(1)} all-gather(bf16[1,1,128]{2,1,0:T(2,128)(2,1)S(1)} %fusion.21), channel_id=2, replica_groups=mesh['narrow'=8,'wide'=32] {'narrow','wide'}, dimensions={0}, use_global_device_ids=true | all-gather | bytes 65792 | tf_op jit(solution)/shard_map/all_gather | solution.py:104
  924.2 5.6 fusion.13
  929.8 5.4 copy.27
  (125 shorter events, 49.2 us)
Async XLA Ops:
  6.5 18.9 %copy-start.1 = (bf16[128,4,16,128]{3,2,1,0:T(8,128)(2,1)S(1)}, bf16[128,4,16,128]{3,2,1,0:T(8,128)(2,1)}, u32[]{:S(2)}) copy-start(bf16[128,4,16,128]{3,2,1,0:T(8,128)(2,1)} %param.9) | copy-start | bytes 6291460
  6.5 9.1 copy-start.2
  6.5 9.2 copy-start.3
  6.5 424.2 %all-reduce.4.cloned.1.call-start = ((), (), s32[]{:S(2)}) async-start(), calls=%async_computation | async-start | bytes 4194304 | tf_op jit(solution)/shard_map/psum | solution.py:101
  9.0 15.3 %collective-permute-start = (bf16[128,1,16,128]{3,0,2,1:T(8,128)(2,1)}, bf16[128,1,16,128]{3,0,2,1:T(8,128)(2,1)}, u32[]{:S(2)}, u32[]{:S(2)}) collective-permute-start(bf16[128,1,16,128]{3,0,2,1:T(8,128)(2,1)} %copy.40), channel_id=1, source_target_pairs={{0,32},{32,64},{64,96},{96,128},{128,160},{160,192},{192,224},{1,3... | collective-permute-start | bytes 1572872 | tf_op jit(solution)/shard_map/ppermute | solution.py:20
  14.3 22.6 %collective-permute-start.1 = (bf16[128,1,16,128]{3,0,2,1:T(8,128)(2,1)S(1)}, bf16[128,1,16,128]{3,0,2,1:T(8,128)(2,1)S(1)}, u32[]{:S(2)}, u32[]{:S(2)}) collective-permute-start(bf16[128,1,16,128]{3,0,2,1:T(8,128)(2,1)S(1)} %copy.41), channel_id=1, source_target_pairs={{32,0},{64,32},{96,64},{128,96},{160,128},{192,160},{224,192},{33,... | collective-permute-start | bytes 1572872 | tf_op jit(solution)/shard_map/ppermute | solution.py:22
  25.4 19.9 %copy-start.4 = (f32[4,4,16,128]{3,2,1,0:T(8,128)S(1)}, f32[4,4,16,128]{3,2,1,0:T(8,128)}, u32[]{:S(2)}) copy-start(f32[4,4,16,128]{3,2,1,0:T(8,128)} %param.11) | copy-start | bytes 393220
  37.0 8.9 collective-permute-start.2
  43.4 10.0 %collective-permute-start.3 = (bf16[128,6,1,128]{3,0,2,1:T(8,128)(2,1)S(1)}, bf16[128,6,1,128]{3,0,2,1:T(8,128)(2,1)S(1)}, u32[]{:S(2)}, u32[]{:S(2)}) collective-permute-start(bf16[128,6,1,128]{3,0,2,1:T(8,128)(2,1)S(1)} %get-tuple-element.192), channel_id=1, source_target_pairs={{1,0},{2,1},{3,2},{4,3},{5,4},{6,5},{7,6},{8,7},{9,8},{10,9},{11,1... | collective-permute-start | bytes 589832 | tf_op jit(solution)/shard_map/ppermute | solution.py:22
  138.5 292.4 %copy-start.5 = (f32[1,4]{1,0:T(1,128)S(1)}, f32[1,4]{1,0:T(1,128)}, u32[]{:S(2)}) copy-start(f32[1,4]{1,0:T(1,128)} %param.14) | copy-start | bytes 52
  138.5 404.8 %all-reduce.6.cloned.1.call-start = ((), (), s32[]{:S(2)}) async-start(), calls=%async_computation.1 | async-start | bytes 4194304 | tf_op jit(solution)/shard_map/psum | solution.py:101
  549.0 27.2 %copy-start = (f32[1024,512]{1,0:T(8,128)S(1)}, f32[1024,512]{1,0:T(8,128)}, u32[]{:S(2)}) copy-start(f32[1024,512]{1,0:T(8,128)} %all-reduce.6.cloned.1.call-done) | copy-start | bytes 6291460
  549.0 375.2 %copy-start.6 = (s32[256]{0:T(256)S(1)}, s32[256]{0:T(256)}, u32[]{:S(2)}) copy-start(s32[256]{0:T(256)} %param.15) | copy-start | bytes 3076
Sparse Core Ops, SparseCore 0:
  138.6 292.1 all-reduce.3
  433.4 109.7 all-reduce.5
